TPU v7x, 256 devices: a whole 4x4x8 slice. The times are simulated.
256 devices in a mesh: grp: 8 (over z), tp: 32 (over x, y, core).
Axes of the slice: x: 4, y: 4, z: 8, core: 2. Of those that a mesh axis runs over, the one named last changes fastest.
Arguments:
- hidden_in: bfloat16 [1024, 3584], P(('grp', 'tp')), may hold values from -6 to 6
- norm_gains: float32 [4, 3584], replicated, may hold values from 0.25 to 1.75
- w_qkv: bfloat16 [3584, 8192], P(None, 'tp'), may hold values from -0.09375 to 0.09375
- w_out: bfloat16 [4096, 3584], P('tp'), may hold values from -0.09375 to 0.09375
- w_gate_up: bfloat16 [2, 3584, 8192], P(None, None, 'tp'), may hold values from -0.09375 to 0.09375
- w_down: bfloat16 [8192, 3584], P('tp'), may hold values from -0.0625 to 0.0625
- prompt_keys: bfloat16 [32768, 2048], P(('grp', 'tp')), may hold values from -480 to 480, as said below
- prompt_values: bfloat16 [32768, 2048], P(('grp', 'tp')), may hold values from -6 to 6
- tail_keys: bfloat16 [1024, 64, 2048], P(('grp', 'tp')), may hold values from -480 to 480, as said below
- tail_values: bfloat16 [1024, 64, 2048], P(('grp', 'tp')), may hold values from -6 to 6
- prompt_len: int32 [80], replicated, may hold values from 1 to 4087, as said below
- group_home: int32 [80], replicated, may hold values from 0 to 7, as said below
- req_group: int32 [1024], P('grp'), may hold values from 0 to 79, as said below
- tail_len: int32 [1024], P('grp'), may hold values from 1 to 64, 32768 in all
Outputs:
- layer_out: bfloat16 [1024, 3584], P(('grp', 'tp'))
Inputs may be any that keep to these rules, and one draw needn't show every extreme that they name: `group_home`: each grp device is home to exactly 10 groups. `prompt_len`: the prompts of the groups homed on one grp device lie one after another in order of group id from the first of that device's 4096 cache positions; together they hold at most 4096 positions, exactly 4096 on one home in every draw, where one group holds 4087 of them. `req_group`: of the 128 requests held by one grp device, at most 32 belong to groups homed on any one grp device; in every draw one home receives exactly 32 requests from every grp device. `prompt_keys`: cached keys, already rotated. `tail_keys`: cached keys, already rotated.
All inputs are finite; a program needn't handle non-finite values. No bound on the sum of `tail_len` on one device may be relied on, other than what follows from the above.
Results may differ from a plain program's by a relative error of at most 0.015.
Values may be sent and summed in bfloat16 or wider, within the bound.
A program may use at most 128 MiB of HBM per device.

v0:
```python
import math
import jax
import jax.numpy as jnp
from jax import lax
from jax.sharding import PartitionSpec as P

HEADS = 16
KV_HEADS = 8
HEAD_DIM = 256
NORM_EPS = 1e-06
SOFT_CAP = 50.0


def rms_scale(values, gain_row):
    values = values.astype(jnp.float32)
    return (
        values * lax.rsqrt(jnp.mean(values * values, axis=-1, keepdims=True) + NORM_EPS) * gain_row
    )


def rotate(head_rows, position):
    half_width = head_rows.shape[-1] // 2
    freq_index = jnp.arange(half_width).astype(jnp.float32)
    frequency = jnp.exp(freq_index * (-math.log(10000.0) / half_width))
    angles = position.astype(jnp.float32)[:, None] * frequency[None, :]
    cosine = jnp.cos(angles)[:, None, :]
    sine_part = jnp.sin(angles)[:, None, :]
    head_rows = head_rows.astype(jnp.float32)
    first_half = head_rows[..., :half_width]
    second = head_rows[..., half_width:]
    return jnp.concatenate(
        [first_half * cosine - second * sine_part, second * cosine + first_half * sine_part],
        axis=-1,
    )


def capped(scores):
    return SOFT_CAP * jnp.tanh(scores * HEAD_DIM ** (-0.5) / SOFT_CAP)


def lookup(lookup_table, index_list):
    matches = index_list[:, None] == jnp.arange(lookup_table.shape[0], dtype=jnp.int32)[None, :]
    return jnp.sum(jnp.where(matches, lookup_table[None, :], 0), axis=1)


def group_starts(prompt_len, group_home):
    group_ids = jnp.arange(prompt_len.shape[0], dtype=jnp.int32)
    same_home = group_home[:, None] == group_home[None, :]
    earlier = group_ids[None, :] < group_ids[:, None]
    return jnp.sum(jnp.where(same_home & earlier, prompt_len[None, :], 0), axis=1)


def shared_part(queries, key_rows, value_rows, visible):
    scores = capped(
        jnp.einsum("nkjd,pkd->nkjp", queries, key_rows, preferred_element_type=jnp.float32)
    )
    exponent = jnp.where(visible[:, None, None, :], jnp.exp(scores), 0.0)
    numerator = jnp.einsum(
        "nkjp,pkd->nkjd",
        exponent.astype(jnp.bfloat16),
        value_rows,
        preferred_element_type=jnp.float32,
    )
    return (numerator, jnp.sum(exponent, axis=-1))


def own_part(queries, key_rows, value_rows, visible):
    scores = capped(
        jnp.einsum("nkjd,npkd->nkjp", queries, key_rows, preferred_element_type=jnp.float32)
    )
    exponent = jnp.where(visible[:, None, None, :], jnp.exp(scores), 0.0)
    numerator = jnp.einsum(
        "nkjp,npkd->nkjd",
        exponent.astype(jnp.bfloat16),
        value_rows,
        preferred_element_type=jnp.float32,
    )
    return (numerator, jnp.sum(exponent, axis=-1))


def per_device(
    hidden_in,
    norm_gains,
    w_qkv,
    w_out,
    w_gate_up,
    w_down,
    prompt_keys,
    prompt_values,
    tail_keys,
    tail_values,
    prompt_len,
    group_home,
    req_group,
    tail_len,
):
    tp_rank = lax.axis_index("tp")
    q_width = HEADS * HEAD_DIM
    kv_width = KV_HEADS * HEAD_DIM
    row_count = hidden_in.shape[0]
    normed = rms_scale(hidden_in, norm_gains[0]).astype(jnp.bfloat16)
    qkv_share = jnp.dot(
        lax.all_gather(normed, "tp", axis=0, tiled=True), w_qkv, preferred_element_type=jnp.float32
    ).astype(jnp.bfloat16)
    projected_qkv = lax.all_gather(qkv_share, "tp", axis=1, tiled=True)
    requests = projected_qkv.shape[0]
    req_len = lookup(prompt_len, req_group)
    position = req_len + tail_len
    queries = rotate(
        projected_qkv[:, :q_width].reshape(requests, HEADS, HEAD_DIM), position
    ).astype(jnp.bfloat16)
    queries = queries.reshape(requests, KV_HEADS, 2, HEAD_DIM)
    key_new = rotate(
        projected_qkv[:, q_width : q_width + kv_width].reshape(requests, KV_HEADS, HEAD_DIM),
        position,
    ).astype(jnp.bfloat16)
    value_new = projected_qkv[:, q_width + kv_width :].reshape(requests, KV_HEADS, HEAD_DIM)
    starts = group_starts(prompt_len, group_home)
    req_home = lookup(group_home, req_group)
    req_start = lookup(starts, req_group)
    cap_dev = prompt_keys.shape[0]
    row_first = tp_rank * row_count
    own_queries = lax.dynamic_slice_in_dim(queries, row_first, row_count, 0)
    own_tail_len = lax.dynamic_slice_in_dim(tail_len, row_first, row_count, 0)
    tail_dev = tail_keys.shape[1]
    tail_pos = jnp.arange(tail_dev, dtype=jnp.int32)
    own_num, own_den = own_part(
        own_queries,
        tail_keys.reshape(row_count, tail_dev, KV_HEADS, HEAD_DIM),
        tail_values.reshape(row_count, tail_dev, KV_HEADS, HEAD_DIM),
        tail_pos[None, :] < own_tail_len[:, None],
    )
    numerator = lax.dynamic_update_slice_in_dim(
        jnp.zeros((requests, KV_HEADS, 2, HEAD_DIM), jnp.float32), own_num, row_first, 0
    )
    denominator = lax.dynamic_update_slice_in_dim(
        jnp.zeros((requests, KV_HEADS, 2), jnp.float32), own_den, row_first, 0
    )
    key_piece = lax.all_gather(prompt_keys, "grp", axis=0, tiled=True)
    value_piece = lax.all_gather(prompt_values, "grp", axis=0, tiled=True)
    piece_rows = key_piece.shape[0]
    gathered_index = jnp.arange(piece_rows, dtype=jnp.int32)
    home_index = gathered_index // cap_dev
    piece_offsets = tp_rank * cap_dev + gathered_index % cap_dev
    visible = (
        (home_index[None, :] == req_home[:, None])
        & (piece_offsets[None, :] >= req_start[:, None])
        & (piece_offsets[None, :] < (req_start + req_len)[:, None])
    )
    part_num, part_den = shared_part(
        queries,
        key_piece.reshape(piece_rows, KV_HEADS, HEAD_DIM),
        value_piece.reshape(piece_rows, KV_HEADS, HEAD_DIM),
        visible,
    )
    numerator, denominator = (numerator + part_num, denominator + part_den)
    share_width = w_out.shape[0]
    first_col = tp_rank * share_width
    flat_num = numerator.reshape(requests, q_width)
    flat_den = denominator.reshape(requests, HEADS)
    total_num, total_den = lax.psum((flat_num, flat_den), "tp")
    share_num = lax.dynamic_slice_in_dim(total_num, first_col, share_width, 1)
    self_exp = jnp.exp(
        capped(jnp.einsum("nkjd,nkd->nkj", queries, key_new, preferred_element_type=jnp.float32))
    )
    self_num = (
        lax.optimization_barrier(self_exp.astype(jnp.bfloat16)).astype(jnp.float32)[..., None]
        * value_new.astype(jnp.float32)[:, :, None, :]
    )
    self_share = lax.dynamic_slice_in_dim(
        self_num.reshape(requests, q_width), first_col, share_width, 1
    )
    total_den = total_den + self_exp.reshape(requests, HEADS)
    head_of_col = (first_col + jnp.arange(share_width, dtype=jnp.int32)) // HEAD_DIM
    head_pick = (head_of_col[None, :] == jnp.arange(HEADS, dtype=jnp.int32)[:, None]).astype(
        jnp.float32
    )
    den_cols = jnp.dot(total_den, head_pick, precision=lax.Precision.HIGHEST)
    attn_share = ((share_num + self_share) / den_cols).astype(jnp.bfloat16)
    block_rows = attn_share
    attn_proj = lax.psum_scatter(
        jnp.dot(block_rows, w_out, preferred_element_type=jnp.float32),
        "tp",
        scatter_dimension=0,
        tiled=True,
    )
    resid = (hidden_in.astype(jnp.float32) + rms_scale(attn_proj, norm_gains[1])).astype(
        jnp.bfloat16
    )
    ffn_in = rms_scale(resid, norm_gains[2]).astype(jnp.bfloat16)
    gate_up = jnp.einsum(
        "rd,kdf->krf",
        lax.all_gather(ffn_in, "tp", axis=0, tiled=True),
        w_gate_up,
        preferred_element_type=jnp.float32,
    )
    hidden_units = (jax.nn.gelu(gate_up[0], approximate=True) * gate_up[1]).astype(jnp.bfloat16)
    block_rows = hidden_units
    ffn_proj = lax.psum_scatter(
        jnp.dot(block_rows, w_down, preferred_element_type=jnp.float32).astype(jnp.bfloat16),
        "tp",
        scatter_dimension=0,
        tiled=True,
    ).astype(jnp.float32)
    return (resid.astype(jnp.float32) + rms_scale(ffn_proj, norm_gains[3])).astype(jnp.bfloat16)


def solution(mesh):
    in_specs = (
        P(("grp", "tp"), None),
        P(),
        P(None, "tp"),
        P("tp", None),
        P(None, None, "tp"),
        P("tp", None),
        P(("grp", "tp"), None),
        P(("grp", "tp"), None),
        P(("grp", "tp"), None, None),
        P(("grp", "tp"), None, None),
        P(),
        P(),
        P("grp"),
        P("grp"),
    )
    out_specs = P(("grp", "tp"), None)
    return jax.shard_map(
        per_device, mesh=mesh, in_specs=in_specs, out_specs=out_specs, check_vma=False
    )
```

profile of v0, /device:TPU:1, one launch (start us, length us, event | category | flops | bytes accessed | tf_op | source)
XLA Modules:
  0.0 625.6 jit_solution(4266515688802575155)
XLA Ops:
  6.5 1.2 slice_reduce_fusion.1
  7.7 0.9 fusion.35
  8.6 0.8 fusion.47
  9.5 26.6 %all-gather = bf16[32,4,3584]{2,1,0:T(4,128)(2,1)S(1)} all-gather(bf16[1,4,3584]{2,1,0:T(4,128)(2,1)S(1)} %fusion.47), channel_id=1, replica_groups=mesh['grp'=8,'tp'=32] {'tp'}, dimensions={0}, use_global_device_ids=true | all-gather | bytes 946176 | tf_op jit(solution)/shard_map/all_gather | solution.py:103
  36.0 1.1 reshape.279
  37.2 2.9 convolution_convert_fusion.1
  40.1 1.0 copy.77
  41.2 1.0 copy.79
  42.3 0.0 all-reduce.6.cloned.1.call-start
  42.3 0.1 dynamic_slice.12
  42.5 0.2 select_reduce_fusion.2
  42.6 0.1 select_reduce_fusion.3
  42.8 0.1 iota_compare_fusion.4
  42.8 0.3 multiply_cosine_fusion
  43.1 0.9 compare_and_fusion
  44.0 46.5 %all-gather.6.cloned.1.call-done = bf16[128,8192]{1,0:T(8,128)(2,1)} async-done(((bf16[128,256]{1,0:T(8,128)(2,1)}), bf16[128,8192]{1,0:T(8,128)(2,1)}) %all-gather.6.cloned.1.call-update) | async-done | bytes 2097168 | tf_op jit(solution)/shard_map/all_gather | solution.py:105
  90.5 1.4 slice_convert_fusion
  91.9 0.7 copy.101
  92.6 0.3 subtract_convert_fusion
  92.9 0.1 copy.75
  93.1 0.1 copy.76
  93.2 0.9 copy-done.11
  94.1 0.5 fusion.73
  94.6 0.1 copy.88
  94.7 2.4 slice_convert_fusion.2
  97.2 0.3 copy.102
  97.5 0.1 subtract_convert_fusion.1
  97.7 0.1 maximum_bitcast_fusion
  97.8 1.2 pad_maximum_fusion
  98.9 0.3 fusion.10
  99.2 50.9 %all-gather.8.cloned.1.call-done = bf16[1024,2048]{0,1:T(8,128)(2,1)} async-done(((bf16[128,2048]{0,1:T(8,128)(2,1)}), bf16[1024,2048]{0,1:T(8,128)(2,1)}) %all-gather.8.cloned.1.call-update) | async-done | bytes 4194320 | tf_op jit(solution)/shard_map/all_gather | solution.py:139
  150.1 7.7 %bitcast_reduce_fusion = (f32[128,8,2]{0,2,1:T(2,128)S(1)}, f32[8,128,2,1024]{3,1,2,0:T(8,128)}) fusion(pred[128,1024]{1,0:T(8,128)(4,1)} %compare_and_fusion, bf16[1024,8,256,1]{0,2,3,1:T(8,128)(2,1)} %bitcast.96, bf16[128,8,2,128]{3,0,2,1:T(8,128)(2,1)S(1)} %bitcast.87, bf16[128,8,2,128]{3,0,2,1:T(8,128)(2,1)S(1)} %bitcast.84), kind=kOutput, calls=%fused_computation | convolution fusion | flops 1084225536 | bytes 13770752 | tf_op jit(solution)/shard_map/nkjd,pkd->nkjp/dot_general | solution.py:55
  157.8 55.1 %all-gather.10.cloned.1.call-done = bf16[1024,2048]{0,1:T(8,128)(2,1)} async-done(((bf16[128,2048]{0,1:T(8,128)(2,1)}), bf16[1024,2048]{0,1:T(8,128)(2,1)}) %all-gather.10.cloned.1.call-update) | async-done | bytes 4194320 | tf_op jit(solution)/shard_map/all_gather | solution.py:140
  212.9 7.0 %fusion = f32[8,128,2,256]{3,1,2,0:T(8,128)S(1)} fusion(bf16[1024,8,256,1]{0,2,3,1:T(8,128)(2,1)} %bitcast.97, f32[8,128,2,1024]{3,1,2,0:T(8,128)} %get-tuple-element.27, pred[128,1024]{1,0:T(8,128)(4,1)} %compare_and_fusion), kind=kOutput, calls=%fused_computation.4 | convolution fusion | flops 1082130432 | bytes 14811136 | tf_op jit(solution)/shard_map/nkjp,pkd->nkjd/dot_general | solution.py:58
  220.0 1.4 copy.123
  221.3 0.7 fusion.28
  222.0 2.9 copy.85
  224.9 2.9 copy.86
  227.8 0.2 all-reduce.8.cloned.1.call-start
  228.1 3.4 fusion.15
  231.4 1.2 copy.94
  232.7 0.2 copy.87
  232.9 0.3 copy.103
  233.3 2.8 broadcast_multiply_fusion
  236.1 4.0 mul.269
  240.1 0.1 dynamic-slice_add_fusion
  240.2 1.3 add.147
  241.4 67.5 %psum.15 = f32[128,16]{0,1:T(8,128)S(1)} all-reduce(f32[128,16]{0,1:T(8,128)S(1)} %bitcast.94), channel_id=1, replica_groups=mesh['grp'=8,'tp'=32] {'tp'}, use_global_device_ids=true, to_apply=%region_8.9 | all-reduce | flops 2048 | bytes 16384 | tf_op jit(solution)/shard_map/psum | solution.py:161
  309.0 38.9 %all-reduce.6.cloned.1.call-done = f32[128,4096]{1,0:T(8,128)} async-done(((f32[128,4096]{1,0:T(8,128)}), f32[128,4096]{1,0:T(8,128)}) %all-reduce.6.cloned.1.call-update) | async-done | bytes 2097168 | tf_op jit(solution)/shard_map/psum | solution.py:161
  347.9 1.1 fusion.5
  349.1 1.6 fusion.74
  350.7 0.0 all-reduce.10.cloned.1.call-start
  350.8 0.6 dynamic-slice.6
  352.0 115.3 %all-reduce.8.cloned.1.call-done = f32[128,3584]{1,0:T(8,128)} async-done(((f32[128,3584]{1,0:T(8,128)}), f32[128,3584]{1,0:T(8,128)}) %all-reduce.8.cloned.1.call-update) | async-done | bytes 1835024
  467.4 1.0 multiply_reduce_fusion
  468.4 1.1 fusion.39
  469.5 0.1 fusion.46
  469.6 28.2 %all-gather.1 = bf16[32,4,3584]{2,1,0:T(4,128)(2,1)} all-gather(bf16[1,4,3584]{2,1,0:T(4,128)(2,1)S(1)} %fusion.46), channel_id=1, replica_groups=mesh['grp'=8,'tp'=32] {'tp'}, dimensions={0}, use_global_device_ids=true | all-gather | bytes 946176 | tf_op jit(solution)/shard_map/all_gather | solution.py:193
  497.9 1.7 reshape.286
  499.5 2.7 convolution_bitcast_fusion
  502.2 1.4 convolution_convert_fusion
  503.7 112.7 %all-reduce.10.cloned.1.call-done = bf16[128,3584]{1,0:T(8,128)(2,1)} async-done(((bf16[128,3584]{1,0:T(8,128)(2,1)}), bf16[128,3584]{1,0:T(8,128)(2,1)}) %all-reduce.10.cloned.1.call-update) | async-done | bytes 917520
  616.3 1.0 fusion.33
  617.3 1.5 fusion.42
  (45 shorter events, 0.4 us)
Async XLA Ops:
  6.5 495.7 %copy-start = (bf16[256,3584]{1,0:T(8,128)(2,1)S(1)}, bf16[256,3584]{1,0:T(8,128)(2,1)}, u32[]{:S(2)}) copy-start(bf16[256,3584]{1,0:T(8,128)(2,1)} %param.19) | copy-start | bytes 5505028
  6.5 83.9 %all-gather.6.cloned.1.call-start = ((), (), s32[]{:S(2)}) async-start(), calls=%async_computation | async-start | bytes 2162688 | tf_op jit(solution)/shard_map/all_gather | solution.py:105
  36.0 4.1 copy-start.4
  37.2 4.0 copy-start.5
  40.0 2.3 copy-start.10
  40.1 2.4 copy-start.7
  40.1 2.4 copy-start.8
  40.1 2.6 copy-start.9
  40.1 110.0 %all-gather.8.cloned.1.call-start = ((), (), s32[]{:S(2)}) async-start(), calls=%async_computation.1 | async-start | bytes 4718592 | tf_op jit(solution)/shard_map/all_gather | solution.py:139
  41.2 171.8 %all-gather.10.cloned.1.call-start = ((), (), s32[]{:S(2)}) async-start(), calls=%async_computation.2 | async-start | bytes 4718592 | tf_op jit(solution)/shard_map/all_gather | solution.py:140
  42.3 305.7 %all-reduce.6.cloned.1.call-start = ((), (), s32[]{:S(2)}) async-start(), calls=%async_computation.3 | async-start | bytes 4194304 | tf_op jit(solution)/shard_map/psum | solution.py:161
  92.9 1.2 copy-start.11
  97.5 1.4 copy-start.2
  227.8 5.1 copy-start.1
  227.8 239.5 %all-reduce.8.cloned.1.call-start = ((), (), s32[]{:S(2)}) async-start(), calls=%async_computation.4 | async-start | bytes 3670016
  236.1 113.0 %copy-start.3 = (bf16[128,3584]{1,0:T(8,128)(2,1)S(1)}, bf16[128,3584]{1,0:T(8,128)(2,1)}, u32[]{:S(2)}) copy-start(bf16[128,3584]{1,0:T(8,128)(2,1)} %param.17) | copy-start | bytes 2752516
  349.1 1.7 copy-start.12
  349.1 119.3 %copy-start.6 = (bf16[4,3584]{1,0:T(4,128)(2,1)S(1)}, bf16[4,3584]{1,0:T(4,128)(2,1)}, u32[]{:S(2)}) copy-start(bf16[4,3584]{1,0:T(4,128)(2,1)} %param.14) | copy-start | bytes 86020
  350.7 265.6 %all-reduce.10.cloned.1.call-start = ((), (), s32[]{:S(2)}) async-start(), calls=%async_computation.5 | async-start | bytes 1835008
Sparse Core Ops, SparseCore 0:
  40.2 50.2 all-gather.5
  92.2 57.8 all-gather.7
  151.8 61.1 all-gather.9
  228.0 119.9 all-reduce.5
  351.1 116.2 all-reduce.7
  503.8 112.4 all-reduce.9
where the time goes:
time: 626 us
  waiting for transfers between devices  419 us (67%)
  blocking collectives  122 us (19%)
  matrix products  28.5 us (5%)
  local copies, waits for them, and re-layouts  23.3 us (4%)
  other arithmetic  17.2 us (3%)
  between operations  14.4 us (2%)
    unnamed x8, waiting for transfers between devices  228 us
    psum x1, blocking collectives, per_device(): total_num, total_den = lax.psum((flat_num, flat_den), 'tp')  67.5 us
    all_gather x1, waiting for transfers between devices, per_device(): value_piece = lax.all_gather(prompt_values, 'grp', axis=0, tiled=True)  55.1 us
    all_gather x1, waiting for transfers between devices, per_device(): key_piece = lax.all_gather(prompt_keys, 'grp', axis=0, tiled=True)  50.9 us
    all_gather x1, waiting for transfers between devices, per_device(): projected_qkv = lax.all_gather(qkv_share, 'tp', axis=1, tiled=True)  46.5 us
    psum x1, waiting for transfers between devices, per_device(): total_num, total_den = lax.psum((flat_num, flat_den), 'tp')  38.9 us
    all_gather x1, blocking collectives, per_device(): lax.all_gather(ffn_in, 'tp', axis=0, tiled=True)  28.2 us
    all_gather x1, blocking collectives, per_device(): lax.all_gather(normed, 'tp', axis=0, tiled=True)  26.6 us
  transfers between devices with their start and end apart: 6, of which 6 were waited for; matrix products, arithmetic and copies ran while one was open for 5% of the time, Pallas kernels for 0%

commit v1 on v0

--- a/solution.py
+++ b/solution.py
@@ -137,7 +137,21 @@
         jnp.zeros((requests, KV_HEADS, 2), jnp.float32), own_den, row_first, 0
     )
     key_piece = lax.all_gather(prompt_keys, "grp", axis=0, tiled=True)
-    value_piece = lax.all_gather(prompt_values, "grp", axis=0, tiled=True)
+    ways, here, step = (lax.axis_size("grp"), lax.axis_index("grp"), prompt_values.shape[0])
+    shape = [n * ways if d == 0 else n for d, n in enumerate(prompt_values.shape)]
+    full = lax.dynamic_update_slice_in_dim(
+        jnp.zeros(shape, prompt_values.dtype), prompt_values, here * step, axis=0
+    )
+    going_up = going_down = prompt_values
+    for far in range(1, ways // 2 + 1):
+        going_up = lax.ppermute(going_up, "grp", [(d, (d + 1) % ways) for d in range(ways)])
+        full = lax.dynamic_update_slice_in_dim(full, going_up, (here - far) % ways * step, axis=0)
+        if 2 * far < ways:
+            going_down = lax.ppermute(going_down, "grp", [(d, (d - 1) % ways) for d in range(ways)])
+            full = lax.dynamic_update_slice_in_dim(
+                full, going_down, (here + far) % ways * step, axis=0
+            )
+    value_piece = full
     piece_rows = key_piece.shape[0]
     gathered_index = jnp.arange(piece_rows, dtype=jnp.int32)
     home_index = gathered_index // cap_dev

time: 626 us -> 577 us (0.922)
  waiting for transfers between devices: 419 us -> 330 us
  local copies, waits for them, and re-layouts: 23.3 us -> 52.2 us
  starting transfers between devices: 0.39 us -> 11.3 us
    all_gather x1 -> x0, waiting for transfers between devices: 55.1 us -> none  [per_device(): value_piece = lax.all_gather(prompt_values, 'grp', axis=0, tiled=True)]
    all_gather x1, waiting for transfers between devices: 46.5 us -> 0.01 us  [per_device(): projected_qkv = lax.all_gather(qkv_share, 'tp', axis=1, tiled=True)]
    ppermute x0 -> x7, waiting for transfers between devices: none -> 26.1 us  [the longest x4 26.1 us: per_device(): lax.ppermute(going_up, 'grp', [(d, (d + 1) % ways) for d in range(ways)])]
    all_gather x1, waiting for transfers between devices: 50.9 us -> 36.6 us  [per_device(): key_piece = lax.all_gather(prompt_keys, 'grp', axis=0, tiled=True)]
    ppermute x0 -> x7, starting transfers between devices: none -> 11.2 us  [the longest x3 9.46 us: per_device(): lax.ppermute(going_down, 'grp', [(d, (d - 1) % ways) for d in range(ways)])]
    add x2, local copies, waits for them, and re-layouts: 4.17 us -> 13.6 us  [per_device(): numerator, denominator = (numerator + part_num, denominator + part_den)]
    dynamic_update_slice x0 -> x8, local copies, waits for them, and re-layouts: none -> 7.12 us  [the longest x4 3.53 us: per_device(): lax.dynamic_update_slice_in_dim(full, going_up, (here - far) % ways * ste...]
    unnamed x8 -> x7, waiting for transfers between devices: 228 us -> 228 us
  transfers between devices with their start and end apart: 6 -> 12, of which waited for: 6 -> 8; matrix products, arithmetic and copies ran while one was open for 5% -> 8% of each run, Pallas kernels for 0% -> 0%
where the time goes in v1:
time: 577 us; the launch traced here: 576 us
  waiting for transfers between devices  330 us (57%)
  blocking collectives  122 us (21%)
  local copies, waits for them, and re-layouts  52.2 us (9%)
  matrix products  24.6 us (4%)
  other arithmetic  20.6 us (4%)
  between operations  14.3 us (2%)
  starting transfers between devices  11.3 us (2%)
    unnamed x7, waiting for transfers between devices  228 us
    psum x1, blocking collectives, per_device(): total_num, total_den = lax.psum((flat_num, flat_den), 'tp')  67.7 us
    psum x1, waiting for transfers between devices, per_device(): total_num, total_den = lax.psum((flat_num, flat_den), 'tp')  39.2 us
    all_gather x1, waiting for transfers between devices, per_device(): key_piece = lax.all_gather(prompt_keys, 'grp', axis=0, tiled=True)  36.6 us
    all_gather x1, blocking collectives, per_device(): lax.all_gather(ffn_in, 'tp', axis=0, tiled=True)  28.2 us
    all_gather x1, blocking collectives, per_device(): lax.all_gather(normed, 'tp', axis=0, tiled=True)  26.6 us
    ppermute x4, waiting for transfers between devices, per_device(): lax.ppermute(going_up, 'grp', [(d, (d + 1) % ways) for d in range(ways)])  26.1 us
    add x2, local copies, waits for them, and re-layouts, per_device(): numerator, denominator = (numerator + part_num, denominator + part_den)  13.6 us
  transfers between devices with their start and end apart: 12, of which 8 were waited for; matrix products, arithmetic and copies ran while one was open for 8% of the time, Pallas kernels for 0%

profile of v1, /device:TPU:1, one launch (start us, length us, event | category | flops | bytes accessed | tf_op | source)
XLA Modules:
  0.0 575.6 jit_solution(2298308670800013352)
XLA Ops:
  6.5 1.8 slice_reduce_fusion.1
  8.4 0.9 fusion.34
  9.3 0.8 fusion.46
  10.1 26.6 %all-gather = bf16[32,4,3584]{2,1,0:T(4,128)(2,1)S(1)} all-gather(bf16[1,4,3584]{2,1,0:T(4,128)(2,1)S(1)} %fusion.46), channel_id=1, replica_groups=mesh['grp'=8,'tp'=32] {'tp'}, dimensions={0}, use_global_device_ids=true | all-gather | bytes 946176 | tf_op jit(solution)/shard_map/all_gather | solution.py:103
  36.7 1.1 reshape.279
  37.8 2.9 convolution_convert_fusion.1
  40.8 1.0 copy.131
  41.9 1.7 collective-permute-start
  43.6 4.0 collective-permute-start.1
  48.3 0.9 select_reduce_fusion.2
  49.3 0.8 select_reduce_fusion.3
  51.1 0.9 compare_and_fusion
  51.9 7.7 %collective-permute-done = bf16[128,2048]{1,0:T(8,128)(2,1)S(1)} collective-permute-done((bf16[128,2048]{1,0:T(8,128)(2,1)S(1)}, bf16[128,2048]{1,0:T(8,128)(2,1)S(1)}, u32[]{:S(2)}, u32[]{:S(2)}) %collective-permute-start) | collective-permute-done | bytes 524320 | tf_op jit(solution)/shard_map/ppermute | solution.py:147
  60.3 2.7 collective-permute-start.3
  63.5 1.3 copy.121
  64.9 2.5 broadcast_in_dim.58
  67.5 0.9 constant_dynamic-update-slice_fusion.7
  68.6 5.1 collective-permute-done.2
  73.7 0.9 constant_dynamic-update-slice_fusion.6
  74.9 2.8 collective-permute-start.5
  77.6 0.9 constant_dynamic-update-slice_fusion.5
  78.5 1.3 copy.124
  79.9 1.3 copy.125
  81.2 0.9 constant_dynamic-update-slice_fusion.4
  82.1 5.1 collective-permute-done.4
  87.1 0.9 constant_dynamic-update-slice_fusion.3
  88.3 1.3 copy.127
  89.6 0.9 constant_dynamic-update-slice_fusion.2
  90.5 0.9 constant_dynamic-update-slice_fusion.1
  91.4 8.2 %collective-permute-done.6 = bf16[128,2048]{1,0:T(8,128)(2,1)} collective-permute-done((bf16[128,2048]{1,0:T(8,128)(2,1)S(1)}, bf16[128,2048]{1,0:T(8,128)(2,1)}, u32[]{:S(2)}, u32[]{:S(2)}) %collective-permute-start.6) | collective-permute-done | bytes 524320 | tf_op jit(solution)/shard_map/ppermute | solution.py:147
  99.6 1.3 copy.128
  100.9 0.9 constant_dynamic-update-slice_fusion
  101.8 1.6 slice_convert_fusion.2
  103.4 1.3 copy.152
  104.7 1.3 copy.151
  108.1 1.1 fusion.72
  109.5 2.0 copy.136
  111.5 1.3 subtract_convert_fusion.1
  112.9 1.1 pad_maximum_fusion
  114.0 36.6 %all-gather.7.cloned.1.call-done = bf16[1024,2048]{0,1:T(8,128)(2,1)} async-done(((bf16[128,2048]{0,1:T(8,128)(2,1)}), bf16[1024,2048]{0,1:T(8,128)(2,1)}) %all-gather.7.cloned.1.call-update) | async-done | bytes 4194320 | tf_op jit(solution)/shard_map/all_gather | solution.py:139
  150.7 5.4 bitcast_reduce_fusion
  156.1 4.8 fusion
  160.9 1.9 bitcast_add_fusion
  162.8 12.3 %add.220 = f32[128,8,2,256]{0,3,2,1:T(8,128)} dynamic-update-slice(f32[128,8,2,256]{0,3,2,1:T(8,128)} %bitcast.77, f32[4,8,2,256]{0,3,2,1:T(8,128)} %bitcast_add_fusion, s32[]{:T(128)S(6)} %select_n.137, s32[]{:T(128)} %constant.118.clone.1, s32[]{:T(128)} %constant.118.clone.1, s32[]{:T(128)} %constant.118.clone.1) | dynamic-update-slice | bytes 131076 | tf_op jit(solution)/shard_map/add | solution.py:170
  175.1 2.9 copy.137
  178.1 3.4 fusion.15
  181.5 1.2 copy.145
  183.0 2.8 broadcast_multiply_fusion
  185.8 4.0 mul.301
  190.0 1.3 add.224
  191.3 67.7 %psum.15 = f32[128,16]{0,1:T(8,128)S(1)} all-reduce(f32[128,16]{0,1:T(8,128)S(1)} %bitcast.92), channel_id=1, replica_groups=mesh['grp'=8,'tp'=32] {'tp'}, use_global_device_ids=true, to_apply=%region_8.9 | all-reduce | flops 2048 | bytes 16384 | tf_op jit(solution)/shard_map/psum | solution.py:175
  259.0 39.2 %all-reduce.6.cloned.1.call-done = f32[128,4096]{1,0:T(8,128)} async-done(((f32[128,4096]{1,0:T(8,128)}), f32[128,4096]{1,0:T(8,128)}) %all-reduce.6.cloned.1.call-update) | async-done | bytes 2097168 | tf_op jit(solution)/shard_map/psum | solution.py:175
  298.2 1.1 fusion.5
  299.3 1.6 fusion.73
  302.2 115.4 %all-reduce.8.cloned.1.call-done = f32[128,3584]{1,0:T(8,128)} async-done(((f32[128,3584]{1,0:T(8,128)}), f32[128,3584]{1,0:T(8,128)}) %all-reduce.8.cloned.1.call-update) | async-done | bytes 1835024
  417.6 1.0 multiply_reduce_fusion
  418.7 1.1 fusion.38
  419.9 28.2 %all-gather.1 = bf16[32,4,3584]{2,1,0:T(4,128)(2,1)} all-gather(bf16[1,4,3584]{2,1,0:T(4,128)(2,1)S(1)} %fusion.45), channel_id=1, replica_groups=mesh['grp'=8,'tp'=32] {'tp'}, dimensions={0}, use_global_device_ids=true | all-gather | bytes 946176 | tf_op jit(solution)/shard_map/all_gather | solution.py:207
  448.1 1.7 reshape.286
  449.8 2.7 convolution_bitcast_fusion
  452.5 1.4 convolution_convert_fusion
  453.9 112.7 %all-reduce.10.cloned.1.call-done = bf16[128,3584]{1,0:T(8,128)(2,1)} async-done(((bf16[128,3584]{1,0:T(8,128)(2,1)}), bf16[128,3584]{1,0:T(8,128)(2,1)}) %all-reduce.10.cloned.1.call-update) | async-done | bytes 917520
  566.6 1.0 fusion.32
  567.6 1.5 fusion.41
  (84 shorter events, 7.5 us)
Async XLA Ops:
  6.5 445.9 %copy-start = (bf16[256,3584]{1,0:T(8,128)(2,1)S(1)}, bf16[256,3584]{1,0:T(8,128)(2,1)}, u32[]{:S(2)}) copy-start(bf16[256,3584]{1,0:T(8,128)(2,1)} %param.19) | copy-start | bytes 5505028
  6.5 34.2 %copy-start.7 = (bf16[128,2048]{1,0:T(8,128)(2,1)S(1)}, bf16[128,2048]{1,0:T(8,128)(2,1)}, u32[]{:S(2)}) copy-start(bf16[128,2048]{1,0:T(8,128)(2,1)} %param.20) | copy-start | bytes 1572868
  6.5 95.2 %all-gather.5.cloned.1.call-start = ((), (), s32[]{:S(2)}) async-start(), calls=%async_computation | async-start | bytes 2162688 | tf_op jit(solution)/shard_map/all_gather | solution.py:105
  37.8 4.1 copy-start.8
  40.7 110.0 %all-gather.7.cloned.1.call-start = ((), (), s32[]{:S(2)}) async-start(), calls=%async_computation.1 | async-start | bytes 4718592 | tf_op jit(solution)/shard_map/all_gather | solution.py:139
  41.8 256.3 %all-reduce.6.cloned.1.call-start = ((), (), s32[]{:S(2)}) async-start(), calls=%async_computation.2 | async-start | bytes 4194304 | tf_op jit(solution)/shard_map/psum | solution.py:175
  41.9 17.8 %collective-permute-start = (bf16[128,2048]{1,0:T(8,128)(2,1)S(1)}, bf16[128,2048]{1,0:T(8,128)(2,1)S(1)}, u32[]{:S(2)}, u32[]{:S(2)}) collective-permute-start(bf16[128,2048]{1,0:T(8,128)(2,1)S(1)} %copy-done.8), channel_id=1, source_target_pairs={{0,32},{32,64},{64,96},{96,128},{128,160},{160,192},{192,224},{224... | collective-permute-start | bytes 1572872 | tf_op jit(solution)/shard_map/ppermute | solution.py:147
  43.6 16.7 %collective-permute-start.1 = (bf16[128,2048]{1,0:T(8,128)(2,1)S(1)}, bf16[128,2048]{1,0:T(8,128)(2,1)S(1)}, u32[]{:S(2)}, u32[]{:S(2)}) collective-permute-start(bf16[128,2048]{1,0:T(8,128)(2,1)S(1)} %copy-done.8), channel_id=1, source_target_pairs={{0,224},{32,0},{64,32},{96,64},{128,96},{160,128},{192,160},{224,1... | collective-permute-start | bytes 1572872 | tf_op jit(solution)/shard_map/ppermute | solution.py:150
  59.7 14.1 %collective-permute-start.2 = (bf16[128,2048]{1,0:T(8,128)(2,1)S(1)}, bf16[128,2048]{1,0:T(8,128)(2,1)}, u32[]{:S(2)}, u32[]{:S(2)}) collective-permute-start(bf16[128,2048]{1,0:T(8,128)(2,1)S(1)} %collective-permute-done), channel_id=1, source_target_pairs={{0,32},{32,64},{64,96},{96,128},{128,160},{160,192},{192,224},{224... | collective-permute-start | bytes 1572872 | tf_op jit(solution)/shard_map/ppermute | solution.py:147
  60.3 14.6 %collective-permute-start.3 = (bf16[128,2048]{1,0:T(8,128)(2,1)S(1)}, bf16[128,2048]{1,0:T(8,128)(2,1)}, u32[]{:S(2)}, u32[]{:S(2)}) collective-permute-start(bf16[128,2048]{1,0:T(8,128)(2,1)S(1)} %collective-permute-done.1), channel_id=1, source_target_pairs={{0,224},{32,0},{64,32},{96,64},{128,96},{160,128},{192,160},{224,1... | collective-permute-start | bytes 1572872 | tf_op jit(solution)/shard_map/ppermute | solution.py:150
  73.7 13.4 %collective-permute-start.4 = (bf16[128,2048]{1,0:T(8,128)(2,1)}, bf16[128,2048]{1,0:T(8,128)(2,1)S(1)}, u32[]{:S(2)}, u32[]{:S(2)}) collective-permute-start(bf16[128,2048]{1,0:T(8,128)(2,1)} %collective-permute-done.2), channel_id=1, source_target_pairs={{0,32},{32,64},{64,96},{96,128},{128,160},{160,192},{192,224},{224... | collective-permute-start | bytes 1572872 | tf_op jit(solution)/shard_map/ppermute | solution.py:147
  74.9 13.4 %collective-permute-start.5 = (bf16[128,2048]{1,0:T(8,128)(2,1)}, bf16[128,2048]{1,0:T(8,128)(2,1)}, u32[]{:S(2)}, u32[]{:S(2)}) collective-permute-start(bf16[128,2048]{1,0:T(8,128)(2,1)} %collective-permute-done.3), channel_id=1, source_target_pairs={{0,224},{32,0},{64,32},{96,64},{128,96},{160,128},{192,160},{224,1... | collective-permute-start | bytes 1572872 | tf_op jit(solution)/shard_map/ppermute | solution.py:150
  87.1 12.5 %collective-permute-start.6 = (bf16[128,2048]{1,0:T(8,128)(2,1)S(1)}, bf16[128,2048]{1,0:T(8,128)(2,1)}, u32[]{:S(2)}, u32[]{:S(2)}) collective-permute-start(bf16[128,2048]{1,0:T(8,128)(2,1)S(1)} %collective-permute-done.4), channel_id=1, source_target_pairs={{0,32},{32,64},{64,96},{96,128},{128,160},{160,192},{192,224},{224... | collective-permute-start | bytes 1572872 | tf_op jit(solution)/shard_map/ppermute | solution.py:147
  101.8 4.2 copy-start.4
  106.9 1.2 copy-start.15
  106.9 1.2 copy-start.18
  106.9 2.3 copy-start.5
  109.2 41.5 %copy-start.10 = (pred[128,1024]{1,0:T(8,128)(4,1)S(1)}, pred[128,1024]{1,0:T(8,128)(4,1)}, u32[]{:S(2)}) copy-start(pred[128,1024]{1,0:T(8,128)(4,1)} %compare_and_fusion) | copy-start | bytes 393220
  156.1 4.8 copy-start.1
  160.9 1.9 copy-start.2
  178.0 4.9 copy-start.3
  178.0 239.6 %all-reduce.8.cloned.1.call-start = ((), (), s32[]{:S(2)}) async-start(), calls=%async_computation.3 | async-start | bytes 3670016
  182.7 7.1 %copy-start.14 = (f32[4,8,2]{2,1,0:T(8,128)S(1)}, f32[4,8,2]{2,1,0:T(8,128)}, u32[]{:S(2)}) copy-start(f32[4,8,2]{2,1,0:T(8,128)} %get-tuple-element.28) | copy-start | bytes 772
  182.7 7.2 %copy-start.13 = (f32[128,8,2]{0,2,1:T(2,128)S(1)}, f32[128,8,2]{0,2,1:T(2,128)}, u32[]{:S(2)}) copy-start(f32[128,8,2]{0,2,1:T(2,128)} %get-tuple-element.26) | copy-start | bytes 24580
  182.7 115.4 %copy-start.17 = (s32[128]{0:T(128)S(1)}, s32[128]{0:T(128)}, u32[]{:S(2)}) copy-start(s32[128]{0:T(128)} %and_select_fusion) | copy-start | bytes 1540
  185.7 113.6 %copy-start.6 = (bf16[128,3584]{1,0:T(8,128)(2,1)S(1)}, bf16[128,3584]{1,0:T(8,128)(2,1)}, u32[]{:S(2)}) copy-start(bf16[128,3584]{1,0:T(8,128)(2,1)} %param.17) | copy-start | bytes 2752516
  185.7 115.3 %copy-start.16 = (u32[256]{0:T(256)S(1)}, u32[256]{0:T(256)}, u32[]{:S(2)}) copy-start(u32[256]{0:T(256)} %constant.151) | copy-start | bytes 3076
  185.7 232.9 %copy-start.9 = (bf16[4,3584]{1,0:T(4,128)(2,1)S(1)}, bf16[4,3584]{1,0:T(4,128)(2,1)}, u32[]{:S(2)}) copy-start(bf16[4,3584]{1,0:T(4,128)(2,1)} %param.14) | copy-start | bytes 86020
  185.7 232.9 %copy-start.12 = (f32[3584]{0:T(1024)S(1)}, f32[3584]{0:T(1024)}, u32[]{:S(2)}) copy-start(f32[3584]{0:T(1024)} %get-tuple-element.6) | copy-start | bytes 43012
  185.8 234.0 %copy-start.11 = (f32[3584]{0:T(1024)S(1)}, f32[3584]{0:T(1024)}, u32[]{:S(2)}) copy-start(f32[3584]{0:T(1024)} %get-tuple-element.5) | copy-start | bytes 43012
  300.9 265.7 %all-reduce.10.cloned.1.call-start = ((), (), s32[]{:S(2)}) async-start(), calls=%async_computation.4 | async-start | bytes 1835008
Sparse Core Ops, SparseCore 0:
  40.8 50.2 all-gather.4
  92.8 57.8 all-gather.6
  178.1 119.9 all-reduce.5
  301.3 116.2 all-reduce.7
  454.0 112.5 all-reduce.9
